TPU v7x, 512 devices: a whole 4x8x8 slice. The times are simulated.
512 devices in a mesh: dp: 4 (over y_hi), ctx: 32 (over z, y_lo, core), head: 4 (over x).
Axes of the slice: x: 4, y: 8 (y_hi: 4, y_lo: 2; y = y_hi * 2 + y_lo), z: 8, core: 2. Of those that a mesh axis runs over, the one named last changes fastest.
Arguments:
- enc_query: bfloat16 [32768, 4096], P(('dp', 'ctx'), 'head'), parts along dimension 0, may hold values from -30 to 30
- enc_key: bfloat16 [32768, 4096], P(('dp', 'ctx'), 'head'), parts along dimension 0, may hold values from -6 to 6
- enc_value: bfloat16 [32768, 4096], P(('dp', 'ctx'), 'head'), parts along dimension 0, may hold values from -6 to 6
- doc_ids: int32 [32768], P(('dp', 'ctx')), parts along dimension 0, may hold values from 0 to 95, never falling along the last dimension, each value on 1 to 256 neighbouring positions
- key_map: bfloat16 [4096, 2048], P('ctx', 'head'), may hold values from -0.09375 to 0.09375
- value_map: bfloat16 [4096, 2048], P('ctx', 'head'), may hold values from -0.09375 to 0.09375
- tgt_query: bfloat16 [8192, 2048], P(('dp', 'ctx'), 'head'), parts along dimension 0, may hold values from -150 to 150
Outputs:
- cross_out: bfloat16 [8192, 2048], P(('dp', 'ctx'), 'head'), parts along dimension 0
There are 4 independent parts, one for each index of `dp`. A program takes and returns all parts, laid end to end along the dimension named above; an argument that names none is the same for every part. Nothing has to cross between parts.
Inputs may be any that keep to these rules, and one draw needn't show every extreme that they name: `doc_ids`: document ids never fall along the pack; each document holds 1 to 256 consecutive positions and one holds exactly 256.
All inputs are finite; a program needn't handle non-finite values.
Results may differ from a plain program's by a relative error of at most 0.011.
Values may be sent and summed in bfloat16 or wider, within the bound.
A program may use at most 64 MiB of HBM per device.

v0:
```python
import jax
import jax.numpy as jnp
from jax import lax
from jax.sharding import PartitionSpec as P

HEAD_DIM = 256
NEG_FILL = -1e30


def passed_along(value, axis, steps):
    count = lax.axis_size(axis)
    leading, last = (max(0, -steps), min(count, count - steps))
    return lax.ppermute(value, axis, [(source, source + steps) for source in range(leading, last)])


def masked_scores(query, keys, query_mark, key_mark):
    scale = query.shape[2] ** (-0.5)
    raw = jnp.einsum("rhe,khe->hrk", query, keys, preferred_element_type=jnp.float32) * scale
    same = query_mark[:, None] == key_mark[None, :]
    return jnp.where(same[None], raw, NEG_FILL)


def weighted(weights, values):
    return jnp.einsum(
        "hrk,khe->rhe", weights.astype(jnp.bfloat16), values, preferred_element_type=jnp.float32
    )


def normalize(summed, total):
    return summed / jnp.transpose(total)[:, :, None]


def dense_attend(query, keys, values, query_mark, key_mark):
    scores = masked_scores(query, keys, query_mark, key_mark)
    top = jnp.max(scores, axis=2, keepdims=True)
    weights = jnp.exp(scores - top)
    return normalize(weighted(weights, values), jnp.sum(weights, axis=2))


def on_device(enc_query, enc_key, enc_value, doc_ids, key_map, value_map, tgt_query):
    head_dim = HEAD_DIM
    heads_here = enc_query.shape[1] // head_dim
    cross_here = key_map.shape[1] // head_dim
    rows = enc_query.shape[0]
    tgt_rows = tgt_query.shape[0]
    query = enc_query.reshape(rows, heads_here, head_dim)
    own_key = enc_key.reshape(rows, heads_here, head_dim)
    own_value = enc_value.reshape(rows, heads_here, head_dim)
    own_mark = (doc_ids + 1).astype(jnp.bfloat16)
    arrived = {}
    for offset in (1, -1):
        arrived[offset] = passed_along((own_key, own_value, own_mark), "ctx", offset)
    left_key, left_value, left_mark = arrived[1]
    right_key, right_value, right_mark = arrived[-1]
    keys = jnp.concatenate([left_key, own_key, right_key], 0)
    values = jnp.concatenate([left_value, own_value, right_value], 0)
    marks = jnp.concatenate([left_mark, own_mark, right_mark], 0)
    enc_out = dense_attend(query, keys, values, own_mark, marks).astype(jnp.bfloat16)
    enc_flat = enc_out.reshape(rows, heads_here * head_dim)
    enc_full = lax.all_gather(enc_flat, "head", axis=1, tiled=True)
    key_sum = jnp.dot(
        enc_full,
        lax.all_gather(key_map, "ctx", axis=0, tiled=True),
        preferred_element_type=jnp.float32,
    )
    value_sum = jnp.dot(
        enc_full,
        lax.all_gather(value_map, "ctx", axis=0, tiled=True),
        preferred_element_type=jnp.float32,
    )
    memory_key = key_sum.astype(jnp.bfloat16).reshape(rows, cross_here, head_dim)
    memory_value = value_sum.astype(jnp.bfloat16).reshape(rows, cross_here, head_dim)
    target = tgt_query.reshape(tgt_rows, cross_here, head_dim)
    target_mark = own_mark.reshape(tgt_rows, rows // tgt_rows)[:, 0]
    near = {}
    for offset in (1, -1):
        near[offset] = passed_along((memory_key, memory_value, own_mark), "ctx", offset)
    keys = jnp.concatenate([near[1][0], memory_key, near[-1][0]], 0)
    values = jnp.concatenate([near[1][1], memory_value, near[-1][1]], 0)
    marks = jnp.concatenate([near[1][2], own_mark, near[-1][2]], 0)
    cross_out = dense_attend(target, keys, values, target_mark, marks)
    return cross_out.astype(jnp.bfloat16).reshape(tgt_rows, cross_here * head_dim)


def solution(mesh):
    in_specs = (
        P(("dp", "ctx"), "head"),
        P(("dp", "ctx"), "head"),
        P(("dp", "ctx"), "head"),
        P(("dp", "ctx")),
        P("ctx", "head"),
        P("ctx", "head"),
        P(("dp", "ctx"), "head"),
    )
    out_specs = P(("dp", "ctx"), "head")
    return jax.shard_map(
        on_device, mesh=mesh, in_specs=in_specs, out_specs=out_specs, check_vma=False
    )
```

profile of v0, /device:TPU:41, one launch (start us, length us, event | category | flops | bytes accessed | tf_op | source)
XLA Modules:
  0.0 251.4 jit_solution(5553337462665344755)
XLA Ops:
  6.5 0.0 all-gather.4.cloned.1.call-start
  6.5 1.3 copy.34
  7.8 0.2 copy.35
  8.1 5.3 %collective-permute-start.4 = (bf16[256,4,256]{2,0,1:T(8,128)(2,1)S(1)}, bf16[256,4,256]{2,0,1:T(8,128)(2,1)S(1)}, u32[]{:S(2)}, u32[]{:S(2)}) collective-permute-start(bf16[256,4,256]{2,0,1:T(8,128)(2,1)S(1)} %copy.35), channel_id=1, source_target_pairs={{0,4},{4,8},{8,12},{12,16},{16,20},{20,24},{24,28},{28,32},{32,36}... | collective-permute-start | bytes 1572872 | tf_op jit(solution)/shard_map/ppermute | solution.py:13
  13.4 1.9 collective-permute-start.5
  15.3 0.7 add_convert_fusion
  16.0 4.5 %collective-permute-start.2 = (bf16[256]{0:T(256)(128)(2,1)S(1)}, bf16[256]{0:T(256)(128)(2,1)S(1)}, u32[]{:S(2)}, u32[]{:S(2)}) collective-permute-start(bf16[256]{0:T(256)(128)(2,1)S(1)} %add_convert_fusion), channel_id=1, source_target_pairs={{0,4},{4,8},{8,12},{12,16},{16,20},{20,24},{24,28},{28,32},{32,36}... | collective-permute-start | bytes 1544 | tf_op jit(solution)/shard_map/ppermute | solution.py:13
  20.6 1.9 collective-permute-start.3
  22.5 1.2 copy.33
  23.7 4.5 %collective-permute-start = (bf16[256,4,256]{0,2,1:T(8,128)(2,1)S(1)}, bf16[256,4,256]{0,2,1:T(8,128)(2,1)S(1)}, u32[]{:S(2)}, u32[]{:S(2)}) collective-permute-start(bf16[256,4,256]{0,2,1:T(8,128)(2,1)S(1)} %bitcast.60), channel_id=1, source_target_pairs={{0,4},{4,8},{8,12},{12,16},{16,20},{20,24},{24,28},{28,32},{32,36}... | collective-permute-start | bytes 1572872 | tf_op jit(solution)/shard_map/ppermute | solution.py:13
  28.3 0.0 collective-permute-done.2
  28.3 1.9 collective-permute-start.1
  30.2 0.0 collective-permute-done.3
  30.3 0.2 broadcast_compare_fusion
  30.4 0.0 collective-permute-done.4
  30.5 0.0 collective-permute-done.5
  30.5 0.7 fusion.2
  31.2 0.7 fusion
  31.8 8.2 %collective-permute-done = bf16[256,4,256]{0,2,1:T(8,128)(2,1)S(1)} collective-permute-done((bf16[256,4,256]{0,2,1:T(8,128)(2,1)S(1)}, bf16[256,4,256]{0,2,1:T(8,128)(2,1)S(1)}, u32[]{:S(2)}, u32[]{:S(2)}) %collective-permute-start) | collective-permute-done | bytes 524320 | tf_op jit(solution)/shard_map/ppermute | solution.py:13
  40.0 0.0 collective-permute-done.1
  40.0 1.9 divide_convert_fusion
  41.9 0.0 all-gather.4.cloned.1.call-update
  41.9 0.0 all-gather.8.cloned.1.call-start
  42.0 0.7 all-gather.8.cloned.1.call-update
  42.7 0.0 all-gather.6.cloned.1.call-start
  42.7 0.7 all-gather.6.cloned.1.call-update
  43.4 0.1 reshape.90
  43.5 0.1 slice_reduce_fusion
  43.6 0.1 broadcast_compare_fusion.1
  43.8 40.8 %all-gather.4.cloned.1.call-done = bf16[256,4096]{0,1:T(8,128)(2,1)} async-done(((bf16[256,1024]{0,1:T(8,128)(2,1)}), bf16[256,4096]{0,1:T(8,128)(2,1)}) %all-gather.4.cloned.1.call-update) | async-done | bytes 2097168 | tf_op jit(solution)/shard_map/all_gather | solution.py:60
  84.5 72.4 %all-gather.8.cloned.1.call-done = bf16[4096,512]{1,0:T(8,128)(2,1)} async-done(((bf16[128,512]{1,0:T(8,128)(2,1)}), bf16[4096,512]{1,0:T(8,128)(2,1)}) %all-gather.8.cloned.1.call-update) | async-done | bytes 4194320 | tf_op jit(solution)/shard_map/all_gather | solution.py:63
  157.0 4.1 %convolution_convert_fusion = bf16[256,512]{1,0:T(8,128)(2,1)S(1)} fusion(bf16[256,4096]{0,1:T(8,128)(2,1)} %all-gather.4.cloned.1.call-done, bf16[4096,512]{1,0:T(8,128)(2,1)} %all-gather.8.cloned.1.call-done), kind=kOutput, calls=%fused_computation.22 | convolution fusion | flops 1073872896 | bytes 6553600 | tf_op jit(solution)/shard_map/dot_general | solution.py:61
  161.1 0.0 copy-start.2
  161.1 3.5 %collective-permute-start.8 = (bf16[256,2,256]{2,0,1:T(8,128)(2,1)S(1)}, bf16[256,2,256]{2,0,1:T(8,128)(2,1)S(1)}, u32[]{:S(2)}, u32[]{:S(2)}) collective-permute-start(bf16[256,2,256]{2,0,1:T(8,128)(2,1)S(1)} %bitcast.64), channel_id=1, source_target_pairs={{0,4},{4,8},{8,12},{12,16},{16,20},{20,24},{24,28},{28,32},{32,36}... | collective-permute-start | bytes 786440 | tf_op jit(solution)/shard_map/ppermute | solution.py:13
  164.6 1.9 collective-permute-start.9
  166.5 62.0 %all-gather.6.cloned.1.call-done = bf16[4096,512]{1,0:T(8,128)(2,1)} async-done(((bf16[128,512]{1,0:T(8,128)(2,1)}), bf16[4096,512]{1,0:T(8,128)(2,1)}) %all-gather.6.cloned.1.call-update) | async-done | bytes 4194320 | tf_op jit(solution)/shard_map/all_gather | solution.py:68
  228.5 0.0 copy-done
  228.5 3.4 %convolution_convert_fusion.1 = bf16[256,512]{1,0:T(8,128)(2,1)S(1)} fusion(bf16[256,4096]{0,1:T(8,128)(2,1)S(1)} %copy-done, bf16[4096,512]{1,0:T(8,128)(2,1)} %all-gather.6.cloned.1.call-done), kind=kOutput, calls=%fused_computation.23 | convolution fusion | flops 1073872896 | bytes 6553600 | tf_op jit(solution)/shard_map/dot_general | solution.py:66
  232.0 3.3 %collective-permute-start.6 = (bf16[256,2,256]{2,0,1:T(8,128)(2,1)S(1)}, bf16[256,2,256]{2,0,1:T(8,128)(2,1)S(1)}, u32[]{:S(2)}, u32[]{:S(2)}) collective-permute-start(bf16[256,2,256]{2,0,1:T(8,128)(2,1)S(1)} %bitcast.67), channel_id=1, source_target_pairs={{0,4},{4,8},{8,12},{12,16},{16,20},{20,24},{24,28},{28,32},{32,36}... | collective-permute-start | bytes 786440 | tf_op jit(solution)/shard_map/ppermute | solution.py:13
  235.3 1.9 collective-permute-start.7
  237.2 0.0 collective-permute-done.8
  237.3 0.0 collective-permute-done.9
  237.3 0.4 select_reduce_fusion
  237.7 0.2 fusion.45
  238.0 0.6 collective-permute-done.6
  238.6 5.3 %collective-permute-done.7 = bf16[256,2,256]{2,0,1:T(8,128)(2,1)S(1)} collective-permute-done((bf16[256,2,256]{2,0,1:T(8,128)(2,1)S(1)}, bf16[256,2,256]{2,0,1:T(8,128)(2,1)S(1)}, u32[]{:S(2)}, u32[]{:S(2)}) %collective-permute-start.7) | collective-permute-done | bytes 262176 | tf_op jit(solution)/shard_map/ppermute | solution.py:13
  243.9 0.4 fusion.28
  244.3 0.6 copy.53
  (7 shorter events, 0.1 us)
Async XLA Ops:
  6.5 23.9 %copy-start.1 = (bf16[256,1024]{1,0:T(8,128)(2,1)S(1)}, bf16[256,1024]{1,0:T(8,128)(2,1)}, u32[]{:S(2)}) copy-start(bf16[256,1024]{1,0:T(8,128)(2,1)} %param.7) | copy-start | bytes 1572868
  6.5 78.0 %all-gather.4.cloned.1.call-start = ((), (), s32[]{:S(2)}) async-start(), calls=%async_computation | async-start | bytes 2621440 | tf_op jit(solution)/shard_map/all_gather | solution.py:60
  8.1 22.4 %collective-permute-start.4 = (bf16[256,4,256]{2,0,1:T(8,128)(2,1)S(1)}, bf16[256,4,256]{2,0,1:T(8,128)(2,1)S(1)}, u32[]{:S(2)}, u32[]{:S(2)}) collective-permute-start(bf16[256,4,256]{2,0,1:T(8,128)(2,1)S(1)} %copy.35), channel_id=1, source_target_pairs={{0,4},{4,8},{8,12},{12,16},{16,20},{20,24},{24,28},{28,32},{32,36}... | collective-permute-start | bytes 1572872 | tf_op jit(solution)/shard_map/ppermute | solution.py:13
  13.4 17.1 %collective-permute-start.5 = (bf16[256,4,256]{2,0,1:T(8,128)(2,1)S(1)}, bf16[256,4,256]{2,0,1:T(8,128)(2,1)S(1)}, u32[]{:S(2)}, u32[]{:S(2)}) collective-permute-start(bf16[256,4,256]{2,0,1:T(8,128)(2,1)S(1)} %copy.35), channel_id=1, source_target_pairs={{4,0},{8,4},{12,8},{16,12},{20,16},{24,20},{28,24},{32,28},{36,32}... | collective-permute-start | bytes 1572872 | tf_op jit(solution)/shard_map/ppermute | solution.py:13
  16.0 12.3 %collective-permute-start.2 = (bf16[256]{0:T(256)(128)(2,1)S(1)}, bf16[256]{0:T(256)(128)(2,1)S(1)}, u32[]{:S(2)}, u32[]{:S(2)}) collective-permute-start(bf16[256]{0:T(256)(128)(2,1)S(1)} %add_convert_fusion), channel_id=1, source_target_pairs={{0,4},{4,8},{8,12},{12,16},{16,20},{20,24},{24,28},{28,32},{32,36}... | collective-permute-start | bytes 1544 | tf_op jit(solution)/shard_map/ppermute | solution.py:13
  20.6 9.7 %collective-permute-start.3 = (bf16[256]{0:T(256)(128)(2,1)S(1)}, bf16[256]{0:T(256)(128)(2,1)S(1)}, u32[]{:S(2)}, u32[]{:S(2)}) collective-permute-start(bf16[256]{0:T(256)(128)(2,1)S(1)} %add_convert_fusion), channel_id=1, source_target_pairs={{4,0},{8,4},{12,8},{16,12},{20,16},{24,20},{28,24},{32,28},{36,32}... | collective-permute-start | bytes 1544 | tf_op jit(solution)/shard_map/ppermute | solution.py:13
  23.7 16.3 %collective-permute-start = (bf16[256,4,256]{0,2,1:T(8,128)(2,1)S(1)}, bf16[256,4,256]{0,2,1:T(8,128)(2,1)S(1)}, u32[]{:S(2)}, u32[]{:S(2)}) collective-permute-start(bf16[256,4,256]{0,2,1:T(8,128)(2,1)S(1)} %bitcast.60), channel_id=1, source_target_pairs={{0,4},{4,8},{8,12},{12,16},{16,20},{20,24},{24,28},{28,32},{32,36}... | collective-permute-start | bytes 1572872 | tf_op jit(solution)/shard_map/ppermute | solution.py:13
  28.3 11.7 %collective-permute-start.1 = (bf16[256,4,256]{0,2,1:T(8,128)(2,1)S(1)}, bf16[256,4,256]{0,2,1:T(8,128)(2,1)S(1)}, u32[]{:S(2)}, u32[]{:S(2)}) collective-permute-start(bf16[256,4,256]{0,2,1:T(8,128)(2,1)S(1)} %bitcast.61), channel_id=1, source_target_pairs={{4,0},{8,4},{12,8},{16,12},{20,16},{24,20},{28,24},{32,28},{36,32}... | collective-permute-start | bytes 1572872 | tf_op jit(solution)/shard_map/ppermute | solution.py:13
  41.9 115.1 %all-gather.8.cloned.1.call-start = ((), (), s32[]{:S(2)}) async-start(), calls=%async_computation.2 | async-start | bytes 4325376 | tf_op jit(solution)/shard_map/all_gather | solution.py:63
  42.7 185.8 %all-gather.6.cloned.1.call-start = ((), (), s32[]{:S(2)}) async-start(), calls=%async_computation.1 | async-start | bytes 4325376 | tf_op jit(solution)/shard_map/all_gather | solution.py:68
  84.5 144.0 %copy-start = (bf16[256,4096]{0,1:T(8,128)(2,1)S(1)}, bf16[256,4096]{0,1:T(8,128)(2,1)}, u32[]{:S(2)}) copy-start(bf16[256,4096]{0,1:T(8,128)(2,1)} %all-gather.4.cloned.1.call-done) | copy-start | bytes 6291460
  161.1 76.2 %copy-start.2 = (bf16[64,512]{1,0:T(8,128)(2,1)S(1)}, bf16[64,512]{1,0:T(8,128)(2,1)}, u32[]{:S(2)}) copy-start(bf16[64,512]{1,0:T(8,128)(2,1)} %param.13) | copy-start | bytes 196612
  161.1 76.1 %collective-permute-start.8 = (bf16[256,2,256]{2,0,1:T(8,128)(2,1)S(1)}, bf16[256,2,256]{2,0,1:T(8,128)(2,1)S(1)}, u32[]{:S(2)}, u32[]{:S(2)}) collective-permute-start(bf16[256,2,256]{2,0,1:T(8,128)(2,1)S(1)} %bitcast.64), channel_id=1, source_target_pairs={{0,4},{4,8},{8,12},{12,16},{16,20},{20,24},{24,28},{28,32},{32,36}... | collective-permute-start | bytes 786440 | tf_op jit(solution)/shard_map/ppermute | solution.py:13
  164.6 72.7 %collective-permute-start.9 = (bf16[256,2,256]{2,0,1:T(8,128)(2,1)S(1)}, bf16[256,2,256]{2,0,1:T(8,128)(2,1)S(1)}, u32[]{:S(2)}, u32[]{:S(2)}) collective-permute-start(bf16[256,2,256]{2,0,1:T(8,128)(2,1)S(1)} %bitcast.65), channel_id=1, source_target_pairs={{4,0},{8,4},{12,8},{16,12},{20,16},{24,20},{28,24},{32,28},{36,32}... | collective-permute-start | bytes 786440 | tf_op jit(solution)/shard_map/ppermute | solution.py:13
  232.0 6.6 %collective-permute-start.6 = (bf16[256,2,256]{2,0,1:T(8,128)(2,1)S(1)}, bf16[256,2,256]{2,0,1:T(8,128)(2,1)S(1)}, u32[]{:S(2)}, u32[]{:S(2)}) collective-permute-start(bf16[256,2,256]{2,0,1:T(8,128)(2,1)S(1)} %bitcast.67), channel_id=1, source_target_pairs={{0,4},{4,8},{8,12},{12,16},{16,20},{20,24},{24,28},{28,32},{32,36}... | collective-permute-start | bytes 786440 | tf_op jit(solution)/shard_map/ppermute | solution.py:13
  235.3 8.6 %collective-permute-start.7 = (bf16[256,2,256]{2,0,1:T(8,128)(2,1)S(1)}, bf16[256,2,256]{2,0,1:T(8,128)(2,1)S(1)}, u32[]{:S(2)}, u32[]{:S(2)}) collective-permute-start(bf16[256,2,256]{2,0,1:T(8,128)(2,1)S(1)} %bitcast.68), channel_id=1, source_target_pairs={{4,0},{8,4},{12,8},{16,12},{20,16},{24,20},{28,24},{32,28},{36,32}... | collective-permute-start | bytes 786440 | tf_op jit(solution)/shard_map/ppermute | solution.py:13
Sparse Core Ops, SparseCore 0:
  42.0 42.4 all-gather.3
  86.7 70.2 all-gather.7
  159.1 69.3 all-gather.5
where the time goes:
time: 252 us; the launch traced here: 251 us
  waiting for transfers between devices  191 us (76%)
  starting transfers between devices  30.9 us (12%)
  between operations  13.3 us (5%)
  matrix products  10.9 us (4%)
  local copies, waits for them, and re-layouts  3.67 us (1%)
    all_gather x1, waiting for transfers between devices, on_device(): lax.all_gather(key_map, 'ctx', axis=0, tiled=True)  72.4 us
    all_gather x1, waiting for transfers between devices, on_device(): lax.all_gather(value_map, 'ctx', axis=0, tiled=True)  62 us
    all_gather x1, waiting for transfers between devices, on_device(): enc_full = lax.all_gather(enc_flat, 'head', axis=1, tiled=True)  40.8 us
    ppermute x10, starting transfers between devices, passed_along(): lax.ppermute(value, axis, [(source, source + steps) for source in range(l...  30.8 us
    ppermute x10, waiting for transfers between devices, passed_along(): lax.ppermute(value, axis, [(source, source + steps) for source in range(l...  14.1 us
  transfers between devices with their start and end apart: 13, of which 6 were waited for; matrix products, arithmetic and copies ran while one was open for 5% of the time, Pallas kernels for 0%

commit v1 on v0

--- a/solution.py
+++ b/solution.py
@@ -60,7 +60,9 @@
     enc_full = lax.all_gather(enc_flat, "head", axis=1, tiled=True)
     key_sum = jnp.dot(
         enc_full,
-        lax.all_gather(key_map, "ctx", axis=0, tiled=True),
+        jnp.concatenate(
+            lax.all_to_all(jnp.stack([key_map] * lax.axis_size("ctx")), "ctx", 0, 0), axis=0
+        ),
         preferred_element_type=jnp.float32,
     )
     value_sum = jnp.dot(

time: 252 us -> 225 us (0.89)
  the two profiles are of different devices: /device:TPU:41 before, /device:TPU:43 now
where the time goes in v1:
time: 225 us; the launch traced here: 224 us
  waiting for transfers between devices  146 us (65%)
  starting transfers between devices  45.7 us (20%)
  between operations  13.7 us (6%)
  matrix products  11.1 us (5%)
  local copies, waits for them, and re-layouts  6.11 us (3%)
    all_to_all x1, waiting for transfers between devices, on_device(): lax.all_to_all(jnp.stack([key_map] * lax.axis_size('ctx')), 'ctx', 0, 0)  85.3 us
    ppermute x10, starting transfers between devices, passed_along(): lax.ppermute(value, axis, [(source, source + steps) for source in range(l...  31.2 us
    all_gather x1, waiting for transfers between devices, on_device(): enc_full = lax.all_gather(enc_flat, 'head', axis=1, tiled=True)  23.6 us
    all_gather x1, waiting for transfers between devices, on_device(): lax.all_gather(value_map, 'ctx', axis=0, tiled=True)  20.7 us
    ppermute x10, waiting for transfers between devices, passed_along(): lax.ppermute(value, axis, [(source, source + steps) for source in range(l...  15.5 us
    all_to_all x1, starting transfers between devices, on_device(): lax.all_to_all(jnp.stack([key_map] * lax.axis_size('ctx')), 'ctx', 0, 0)  14.5 us
  transfers between devices with their start and end apart: 13, of which 6 were waited for; matrix products, arithmetic and copies ran while one was open for 7% of the time, Pallas kernels for 0%

profile of v1, /device:TPU:43, one launch (start us, length us, event | category | flops | bytes accessed | tf_op | source)
XLA Modules:
  0.0 224.3 jit_solution(5049327425931422664)
XLA Ops:
  6.5 0.0 all-gather.3.cloned.1.call-start
  6.5 1.3 copy.34
  7.8 0.2 copy.35
  8.1 5.3 %collective-permute-start.4 = (bf16[256,4,256]{2,0,1:T(8,128)(2,1)S(1)}, bf16[256,4,256]{2,0,1:T(8,128)(2,1)S(1)}, u32[]{:S(2)}, u32[]{:S(2)}) collective-permute-start(bf16[256,4,256]{2,0,1:T(8,128)(2,1)S(1)} %copy.35), channel_id=1, source_target_pairs={{0,4},{4,8},{8,12},{12,16},{16,20},{20,24},{24,28},{28,32},{32,36}... | collective-permute-start | bytes 1572872 | tf_op jit(solution)/shard_map/ppermute | solution.py:13
  13.4 1.9 collective-permute-start.5
  15.3 0.7 add_convert_fusion
  16.0 4.5 %collective-permute-start.2 = (bf16[256]{0:T(256)(128)(2,1)S(1)}, bf16[256]{0:T(256)(128)(2,1)S(1)}, u32[]{:S(2)}, u32[]{:S(2)}) collective-permute-start(bf16[256]{0:T(256)(128)(2,1)S(1)} %add_convert_fusion), channel_id=1, source_target_pairs={{0,4},{4,8},{8,12},{12,16},{16,20},{20,24},{24,28},{28,32},{32,36}... | collective-permute-start | bytes 1544 | tf_op jit(solution)/shard_map/ppermute | solution.py:13
  20.6 1.9 collective-permute-start.3
  22.5 1.2 copy.33
  23.7 4.5 %collective-permute-start = (bf16[256,4,256]{0,2,1:T(8,128)(2,1)S(1)}, bf16[256,4,256]{0,2,1:T(8,128)(2,1)S(1)}, u32[]{:S(2)}, u32[]{:S(2)}) collective-permute-start(bf16[256,4,256]{0,2,1:T(8,128)(2,1)S(1)} %bitcast.61), channel_id=1, source_target_pairs={{0,4},{4,8},{8,12},{12,16},{16,20},{20,24},{24,28},{28,32},{32,36}... | collective-permute-start | bytes 1572872 | tf_op jit(solution)/shard_map/ppermute | solution.py:13
  28.3 0.0 collective-permute-done.2
  28.3 1.9 collective-permute-start.1
  30.2 0.0 collective-permute-done.3
  30.3 0.2 broadcast_compare_fusion
  30.4 0.0 collective-permute-done.4
  30.5 0.0 collective-permute-done.5
  30.5 0.0 copy-done.2
  30.5 0.7 fusion.2
  31.2 0.7 fusion
  31.8 8.2 %collective-permute-done = bf16[256,4,256]{0,2,1:T(8,128)(2,1)S(1)} collective-permute-done((bf16[256,4,256]{0,2,1:T(8,128)(2,1)S(1)}, bf16[256,4,256]{0,2,1:T(8,128)(2,1)S(1)}, u32[]{:S(2)}, u32[]{:S(2)}) %collective-permute-start) | collective-permute-done | bytes 524320 | tf_op jit(solution)/shard_map/ppermute | solution.py:13
  40.0 0.0 collective-permute-done.1
  40.0 1.9 divide_convert_fusion
  41.9 0.0 all-gather.3.cloned.1.call-update
  41.9 2.4 %stack.2 = bf16[32,128,512]{2,1,0:T(8,128)(2,1)} broadcast(bf16[128,512]{1,0:T(8,128)(2,1)S(1)} %copy-done), dimensions={1,2} | broadcast | bytes 4325376 | tf_op jit(solution)/shard_map/stack | solution.py:64
  44.4 14.5 %all-to-all-start = ((bf16[32,128,512]{2,1,0:T(8,128)(2,1)}), bf16[32,128,512]{2,1,0:T(8,128)(2,1)}, u32[]{:S(2)}, u32[]{:S(2)}) async-start(bf16[32,128,512]{2,1,0:T(8,128)(2,1)} %stack.2), calls=%async_computation | async-start | bytes 8388608 | tf_op jit(solution)/shard_map/all_to_all | solution.py:64
  58.9 0.0 all-gather.5.cloned.1.call-start
  58.9 0.7 all-gather.5.cloned.1.call-update
  59.6 0.1 reshape.95
  59.7 0.1 slice_reduce_fusion
  59.9 0.1 broadcast_compare_fusion.1
  60.0 23.6 %all-gather.3.cloned.1.call-done = bf16[256,4096]{0,1:T(8,128)(2,1)} async-done(((bf16[256,1024]{0,1:T(8,128)(2,1)}), bf16[256,4096]{0,1:T(8,128)(2,1)}) %all-gather.3.cloned.1.call-update) | async-done | bytes 2097168 | tf_op jit(solution)/shard_map/all_gather | solution.py:60
  83.6 85.3 %all-to-all-done = bf16[32,128,512]{2,1,0:T(8,128)(2,1)} async-done(((bf16[32,128,512]{2,1,0:T(8,128)(2,1)}), bf16[32,128,512]{2,1,0:T(8,128)(2,1)}, u32[]{:S(2)}, u32[]{:S(2)}) %all-to-all-start) | async-done | bytes 4194336 | tf_op jit(solution)/shard_map/all_to_all | solution.py:64
  168.9 4.3 %convolution_convert_fusion = bf16[256,512]{1,0:T(8,128)(2,1)S(1)} fusion(bf16[256,4096]{0,1:T(8,128)(2,1)} %all-gather.3.cloned.1.call-done, bf16[4096,512]{1,0:T(8,128)(2,1)} %bitcast.6), kind=kOutput, calls=%fused_computation.22 | convolution fusion | flops 1073872896 | bytes 6553600 | tf_op jit(solution)/shard_map/dot_general | solution.py:61
  173.2 0.0 copy-start.3
  173.2 2.1 collective-permute-start.8
  175.3 4.6 %collective-permute-start.9 = (bf16[256,2,256]{2,0,1:T(8,128)(2,1)S(1)}, bf16[256,2,256]{2,0,1:T(8,128)(2,1)S(1)}, u32[]{:S(2)}, u32[]{:S(2)}) collective-permute-start(bf16[256,2,256]{2,0,1:T(8,128)(2,1)S(1)} %bitcast.66), channel_id=1, source_target_pairs={{4,0},{8,4},{12,8},{16,12},{20,16},{24,20},{28,24},{32,28},{36,32}... | collective-permute-start | bytes 786440 | tf_op jit(solution)/shard_map/ppermute | solution.py:13
  179.9 20.7 %all-gather.5.cloned.1.call-done = bf16[4096,512]{1,0:T(8,128)(2,1)} async-done(((bf16[128,512]{1,0:T(8,128)(2,1)}), bf16[4096,512]{1,0:T(8,128)(2,1)}) %all-gather.5.cloned.1.call-update) | async-done | bytes 4194320 | tf_op jit(solution)/shard_map/all_gather | solution.py:70
  200.6 3.4 %convolution_convert_fusion.1 = bf16[256,512]{1,0:T(8,128)(2,1)S(1)} fusion(bf16[256,4096]{0,1:T(8,128)(2,1)S(1)} %copy-done.1, bf16[4096,512]{1,0:T(8,128)(2,1)} %all-gather.5.cloned.1.call-done), kind=kOutput, calls=%fused_computation.23 | convolution fusion | flops 1073872896 | bytes 6553600 | tf_op jit(solution)/shard_map/dot_general | solution.py:68
  204.1 1.9 collective-permute-start.6
  206.0 2.4 %collective-permute-start.7 = (bf16[256,2,256]{2,0,1:T(8,128)(2,1)S(1)}, bf16[256,2,256]{2,0,1:T(8,128)(2,1)S(1)}, u32[]{:S(2)}, u32[]{:S(2)}) collective-permute-start(bf16[256,2,256]{2,0,1:T(8,128)(2,1)S(1)} %bitcast.69), channel_id=1, source_target_pairs={{4,0},{8,4},{12,8},{16,12},{20,16},{24,20},{28,24},{32,28},{36,32}... | collective-permute-start | bytes 786440 | tf_op jit(solution)/shard_map/ppermute | solution.py:13
  208.4 0.0 collective-permute-done.8
  208.4 0.0 collective-permute-done.9
  208.4 0.4 select_reduce_fusion
  208.9 0.2 fusion.45
  209.1 0.2 collective-permute-done.6
  209.3 7.2 %collective-permute-done.7 = bf16[256,2,256]{2,0,1:T(8,128)(2,1)S(1)} collective-permute-done((bf16[256,2,256]{2,0,1:T(8,128)(2,1)S(1)}, bf16[256,2,256]{2,0,1:T(8,128)(2,1)S(1)}, u32[]{:S(2)}, u32[]{:S(2)}) %collective-permute-start.7) | collective-permute-done | bytes 262176 | tf_op jit(solution)/shard_map/ppermute | solution.py:13
  216.5 0.4 fusion.28
  216.8 0.6 copy.53
  (9 shorter events, 0.1 us)
Async XLA Ops:
  6.5 23.9 %copy-start.2 = (bf16[256,1024]{1,0:T(8,128)(2,1)S(1)}, bf16[256,1024]{1,0:T(8,128)(2,1)}, u32[]{:S(2)}) copy-start(bf16[256,1024]{1,0:T(8,128)(2,1)} %param.7) | copy-start | bytes 1572868
  6.5 77.0 %all-gather.3.cloned.1.call-start = ((), (), s32[]{:S(2)}) async-start(), calls=%async_computation.1 | async-start | bytes 2621440 | tf_op jit(solution)/shard_map/all_gather | solution.py:60
  8.1 22.4 %collective-permute-start.4 = (bf16[256,4,256]{2,0,1:T(8,128)(2,1)S(1)}, bf16[256,4,256]{2,0,1:T(8,128)(2,1)S(1)}, u32[]{:S(2)}, u32[]{:S(2)}) collective-permute-start(bf16[256,4,256]{2,0,1:T(8,128)(2,1)S(1)} %copy.35), channel_id=1, source_target_pairs={{0,4},{4,8},{8,12},{12,16},{16,20},{20,24},{24,28},{28,32},{32,36}... | collective-permute-start | bytes 1572872 | tf_op jit(solution)/shard_map/ppermute | solution.py:13
  13.4 17.1 %collective-permute-start.5 = (bf16[256,4,256]{2,0,1:T(8,128)(2,1)S(1)}, bf16[256,4,256]{2,0,1:T(8,128)(2,1)S(1)}, u32[]{:S(2)}, u32[]{:S(2)}) collective-permute-start(bf16[256,4,256]{2,0,1:T(8,128)(2,1)S(1)} %copy.35), channel_id=1, source_target_pairs={{4,0},{8,4},{12,8},{16,12},{20,16},{24,20},{28,24},{32,28},{36,32}... | collective-permute-start | bytes 1572872 | tf_op jit(solution)/shard_map/ppermute | solution.py:13
  16.0 12.3 %collective-permute-start.2 = (bf16[256]{0:T(256)(128)(2,1)S(1)}, bf16[256]{0:T(256)(128)(2,1)S(1)}, u32[]{:S(2)}, u32[]{:S(2)}) collective-permute-start(bf16[256]{0:T(256)(128)(2,1)S(1)} %add_convert_fusion), channel_id=1, source_target_pairs={{0,4},{4,8},{8,12},{12,16},{16,20},{20,24},{24,28},{28,32},{32,36}... | collective-permute-start | bytes 1544 | tf_op jit(solution)/shard_map/ppermute | solution.py:13
  20.6 9.7 %collective-permute-start.3 = (bf16[256]{0:T(256)(128)(2,1)S(1)}, bf16[256]{0:T(256)(128)(2,1)S(1)}, u32[]{:S(2)}, u32[]{:S(2)}) collective-permute-start(bf16[256]{0:T(256)(128)(2,1)S(1)} %add_convert_fusion), channel_id=1, source_target_pairs={{4,0},{8,4},{12,8},{16,12},{20,16},{24,20},{28,24},{32,28},{36,32}... | collective-permute-start | bytes 1544 | tf_op jit(solution)/shard_map/ppermute | solution.py:13
  23.7 16.3 %collective-permute-start = (bf16[256,4,256]{0,2,1:T(8,128)(2,1)S(1)}, bf16[256,4,256]{0,2,1:T(8,128)(2,1)S(1)}, u32[]{:S(2)}, u32[]{:S(2)}) collective-permute-start(bf16[256,4,256]{0,2,1:T(8,128)(2,1)S(1)} %bitcast.61), channel_id=1, source_target_pairs={{0,4},{4,8},{8,12},{12,16},{16,20},{20,24},{24,28},{28,32},{32,36}... | collective-permute-start | bytes 1572872 | tf_op jit(solution)/shard_map/ppermute | solution.py:13
  28.3 11.7 %collective-permute-start.1 = (bf16[256,4,256]{0,2,1:T(8,128)(2,1)S(1)}, bf16[256,4,256]{0,2,1:T(8,128)(2,1)S(1)}, u32[]{:S(2)}, u32[]{:S(2)}) collective-permute-start(bf16[256,4,256]{0,2,1:T(8,128)(2,1)S(1)} %bitcast.62), channel_id=1, source_target_pairs={{4,0},{8,4},{12,8},{16,12},{20,16},{24,20},{28,24},{32,28},{36,32}... | collective-permute-start | bytes 1572872 | tf_op jit(solution)/shard_map/ppermute | solution.py:13
  40.0 1.9 copy-start
  44.4 124.5 %all-to-all-start = ((bf16[32,128,512]{2,1,0:T(8,128)(2,1)}), bf16[32,128,512]{2,1,0:T(8,128)(2,1)}, u32[]{:S(2)}, u32[]{:S(2)}) async-start(bf16[32,128,512]{2,1,0:T(8,128)(2,1)} %stack.2), calls=%async_computation | async-start | bytes 8388608 | tf_op jit(solution)/shard_map/all_to_all | solution.py:64
  58.9 141.7 %all-gather.5.cloned.1.call-start = ((), (), s32[]{:S(2)}) async-start(), calls=%async_computation.2 | async-start | bytes 4325376 | tf_op jit(solution)/shard_map/all_gather | solution.py:70
  168.9 31.7 %copy-start.1 = (bf16[256,4096]{0,1:T(8,128)(2,1)S(1)}, bf16[256,4096]{0,1:T(8,128)(2,1)}, u32[]{:S(2)}) copy-start(bf16[256,4096]{0,1:T(8,128)(2,1)} %all-gather.3.cloned.1.call-done) | copy-start | bytes 6291460
  173.2 35.2 %copy-start.3 = (bf16[64,512]{1,0:T(8,128)(2,1)S(1)}, bf16[64,512]{1,0:T(8,128)(2,1)}, u32[]{:S(2)}) copy-start(bf16[64,512]{1,0:T(8,128)(2,1)} %param.13) | copy-start | bytes 196612
  173.2 35.2 %collective-permute-start.8 = (bf16[256,2,256]{2,0,1:T(8,128)(2,1)S(1)}, bf16[256,2,256]{2,0,1:T(8,128)(2,1)S(1)}, u32[]{:S(2)}, u32[]{:S(2)}) collective-permute-start(bf16[256,2,256]{2,0,1:T(8,128)(2,1)S(1)} %bitcast.65), channel_id=1, source_target_pairs={{0,4},{4,8},{8,12},{12,16},{16,20},{20,24},{24,28},{28,32},{32,36}... | collective-permute-start | bytes 786440 | tf_op jit(solution)/shard_map/ppermute | solution.py:13
  175.3 33.1 %collective-permute-start.9 = (bf16[256,2,256]{2,0,1:T(8,128)(2,1)S(1)}, bf16[256,2,256]{2,0,1:T(8,128)(2,1)S(1)}, u32[]{:S(2)}, u32[]{:S(2)}) collective-permute-start(bf16[256,2,256]{2,0,1:T(8,128)(2,1)S(1)} %bitcast.66), channel_id=1, source_target_pairs={{4,0},{8,4},{12,8},{16,12},{20,16},{24,20},{28,24},{32,28},{36,32}... | collective-permute-start | bytes 786440 | tf_op jit(solution)/shard_map/ppermute | solution.py:13
  204.1 5.2 %collective-permute-start.6 = (bf16[256,2,256]{2,0,1:T(8,128)(2,1)S(1)}, bf16[256,2,256]{2,0,1:T(8,128)(2,1)S(1)}, u32[]{:S(2)}, u32[]{:S(2)}) collective-permute-start(bf16[256,2,256]{2,0,1:T(8,128)(2,1)S(1)} %bitcast.68), channel_id=1, source_target_pairs={{0,4},{4,8},{8,12},{12,16},{16,20},{20,24},{24,28},{28,32},{32,36}... | collective-permute-start | bytes 786440 | tf_op jit(solution)/shard_map/ppermute | solution.py:13
  206.0 10.5 %collective-permute-start.7 = (bf16[256,2,256]{2,0,1:T(8,128)(2,1)S(1)}, bf16[256,2,256]{2,0,1:T(8,128)(2,1)S(1)}, u32[]{:S(2)}, u32[]{:S(2)}) collective-permute-start(bf16[256,2,256]{2,0,1:T(8,128)(2,1)S(1)} %bitcast.69), channel_id=1, source_target_pairs={{4,0},{8,4},{12,8},{16,12},{20,16},{24,20},{28,24},{32,28},{36,32}... | collective-permute-start | bytes 786440 | tf_op jit(solution)/shard_map/ppermute | solution.py:13
Sparse Core Ops, SparseCore 0:
  42.0 41.4 all-gather.2
  85.7 114.8 all-gather.4
